TPU v7x, 512 devices: a whole 4x8x8 slice. The times are simulated.
512 devices in a mesh: sec: 2 (over y_lo), exp: 32 (over y_hi, x, core), hid: 8 (over z).
Axes of the slice: x: 4, y: 8 (y_hi: 4, y_lo: 2; y = y_hi * 2 + y_lo), z: 8, core: 2. Of those that a mesh axis runs over, the one named last changes fastest.
Arguments:
- tokens: bfloat16 [1024, 4096], P('exp', ('sec', 'hid')), may hold values from -1200 to 1200
- norm_gain: bfloat16 [4096], P(('sec', 'hid')), may hold values from 0.5 to 2
- route_weight: float32 [1024, 2], P('exp'), may hold values from 0.1 to 1
- block_experts: int32 [8, 2], replicated, may hold values from 0 to 7, all different within a row; in each aligned block of 8 rows (0 to 7, 8 to 15, ...) at most 4 rows name the same one
- w_gate: bfloat16 [2, 4096, 32768], P('sec', None, ('exp', 'hid')), may hold values from -0.09375 to 0.09375
- w_up: bfloat16 [2, 4096, 32768], P('sec', None, ('exp', 'hid')), may hold values from -0.09375 to 0.09375
- w_down: bfloat16 [2, 32768, 4096], P('sec', ('exp', 'hid')), may hold values from -0.0625 to 0.0625
Outputs:
- moe_out: bfloat16 [1024, 4096], P('exp', ('sec', 'hid'))
Inputs may be any that keep to these rules, and one draw needn't show every extreme that they name: `block_experts`: each row names 2 different experts; no expert is named by more than 4 rows, a bound that some block reaches; every expert is named by some row.
All inputs are finite; a program needn't handle non-finite values.
Results may differ from a plain program's by a relative error of at most 0.018.
Values may be sent and summed in bfloat16 or wider, within the bound.
No kernel may reach another device: no remote copies, remote signals or barrier semaphores. Data moves between devices by JAX's collectives and lax.ppermute only.
A program may use at most 64 MiB of HBM per device.

v0:
```python
import jax
import jax.numpy as jnp
from jax import lax
from jax.sharding import PartitionSpec as P

D = 4096
EXPERTS = 8
BLK = 128
MOST = 4


def per_device(tokens, norm_gain, route_weight, block_experts, w_gate, w_up, w_down):
    exp_devices = lax.axis_size("exp")
    group_size = exp_devices // EXPERTS
    my_expert = lax.axis_index("exp") // group_size
    tok_local = tokens.shape[0]
    total_rows = tok_local * exp_devices
    num_blocks = total_rows // BLK
    slot_count = MOST
    gate_local = w_gate[0]
    up_local = w_up[0]
    down_local = w_down[0]
    block_hit = jnp.any(block_experts == my_expert, axis=1)
    hit_flags = block_hit.astype(jnp.int32)
    slot_of_block = jnp.where(block_hit, jnp.cumsum(hit_flags) - 1, -1)
    slot_ids = jnp.arange(slot_count, dtype=jnp.int32)
    slot_match = slot_of_block[None, :] == slot_ids[:, None]
    block_ids = jnp.arange(num_blocks, dtype=jnp.int32)
    block_of_slot = jnp.sum(jnp.where(slot_match, block_ids[None, :], 0), axis=1)
    slot_valid = jnp.any(slot_match, axis=1)
    values = tokens.astype(jnp.float32)
    square_part = jnp.sum(values * values, axis=1)
    square_total = lax.psum(square_part, ("sec", "hid"))
    rms_value = jnp.sqrt(square_total / D + 1e-05)
    normed = (values * norm_gain.astype(jnp.float32) / rms_value[:, None]).astype(jnp.bfloat16)
    gathered = lax.all_gather(normed, "exp", axis=0, tiled=True)
    width = gathered.shape[1]
    picked = jnp.take(gathered.reshape(num_blocks, BLK, width), block_of_slot, axis=0)
    picked = jnp.where(slot_valid[:, None, None], picked, jnp.zeros_like(picked))
    picked_rows = picked.reshape(slot_count * BLK, width)
    feature_piece = lax.all_gather(picked_rows, ("sec", "hid"), axis=1, tiled=True)
    gate_acc = jnp.dot(feature_piece, gate_local, preferred_element_type=jnp.float32)
    up_acc = jnp.dot(feature_piece, up_local, preferred_element_type=jnp.float32)
    activated = (jax.nn.silu(gate_acc) * up_acc).astype(jnp.bfloat16)
    contribution = jnp.dot(activated, down_local, preferred_element_type=jnp.float32)
    term_vals = contribution.astype(jnp.bfloat16)
    own_rows = lax.axis_index("exp") * tok_local + jnp.arange(tok_local, dtype=jnp.int32)
    own_blocks = own_rows // BLK
    own_experts = jnp.take(block_experts, own_blocks, axis=0)
    source_expert = jnp.arange(exp_devices, dtype=jnp.int32) // group_size
    factor = jnp.sum(
        jnp.where(
            own_experts[None, :, :] == source_expert[:, None, None], route_weight[None, :, :], 0.0
        ),
        axis=2,
    )
    reduced = lax.psum_scatter(term_vals, ("sec", "hid"), scatter_dimension=1, tiled=True).astype(
        jnp.float32
    )
    width = reduced.shape[1]
    slot_grid = reduced.reshape(slot_count, BLK, width)
    safe_slot = jnp.maximum(slot_of_block, 0)
    expanded = jnp.take(slot_grid, safe_slot, axis=0)
    expanded = jnp.where(block_hit[:, None, None], expanded, jnp.zeros_like(expanded))
    outgoing = expanded.reshape(exp_devices, tok_local, width)
    received = lax.all_to_all(
        outgoing.astype(jnp.bfloat16), "exp", split_axis=0, concat_axis=0, tiled=True
    ).astype(outgoing.dtype)
    result = jnp.sum(received * factor[:, :, None], axis=0)
    return result.astype(jnp.bfloat16)


def solution(mesh):
    return jax.shard_map(
        per_device,
        mesh=mesh,
        in_specs=(
            P("exp", ("sec", "hid")),
            P(("sec", "hid")),
            P("exp", None),
            P(),
            P("sec", None, ("exp", "hid")),
            P("sec", None, ("exp", "hid")),
            P("sec", ("exp", "hid"), None),
        ),
        out_specs=P("exp", ("sec", "hid")),
        check_vma=False,
    )
```

profile of v0, /device:TPU:9, one launch (start us, length us, event | category | flops | bytes accessed | tf_op | source)
XLA Modules:
  0.0 313.3 jit_solution(5382523622550973638)
XLA Ops:
  6.5 0.8 compare_reduce_fusion
  7.4 0.2 reduce-window.4
  7.6 0.1 select_reduce_fusion.1
  7.7 0.1 fusion.16
  7.9 0.8 fusion.15
  8.7 32.5 %psum.7 = f32[32]{0:T(128)S(1)} all-reduce(f32[32]{0:T(128)S(1)} %fusion.15), channel_id=1, replica_groups=mesh['sec'=2,'exp'=32,'hid'=8] {'sec','hid'}, use_global_device_ids=true, to_apply=%region_5.6 | all-reduce | flops 32 | bytes 256 | tf_op jit(solution)/shard_map/psum | solution.py:33
  41.2 0.7 convert_element_type.37
  41.9 0.8 fusion.14
  42.7 54.8 %all_gather.6 = bf16[1024,256]{1,0:T(8,128)(2,1)S(1)} all-gather(bf16[32,256]{1,0:T(8,128)(2,1)S(1)} %fusion.14), channel_id=1, replica_groups=mesh['sec'=2,'exp'=32,'hid'=8] {'exp'}, dimensions={0}, use_global_device_ids=true | all-gather | bytes 540672 | tf_op jit(solution)/shard_map/all_gather | solution.py:36
  97.4 0.6 gather_fusion
  98.1 0.9 fusion.6
  99.1 70.2 %all-gather.2.cloned.1.call-done = bf16[512,4096]{1,0:T(8,128)(2,1)} async-done(((bf16[512,256]{1,0:T(8,128)(2,1)}), bf16[512,4096]{1,0:T(8,128)(2,1)}) %all-gather.2.cloned.1.call-update) | async-done | bytes 4194320 | tf_op jit(solution)/shard_map/all_gather | solution.py:41
  169.3 3.7 %fusion.4 = f32[512,128]{1,0:T(8,128)S(1)} fusion(bf16[512,4096]{1,0:T(8,128)(2,1)} %all-gather.2.cloned.1.call-done, bf16[1,4096,128]{2,1,0:T(8,128)(2,1)} %param.11), kind=kOutput, calls=%fused_computation.8 | convolution fusion | flops 536870912 | bytes 5505024 | tf_op jit(solution)/shard_map/dot_general | solution.py:42
  173.1 8.6 %convolution_convert_fusion = bf16[512,4096]{1,0:T(8,128)(2,1)} fusion(bf16[512,4096]{1,0:T(8,128)(2,1)} %all-gather.2.cloned.1.call-done, bf16[1,128,4096]{2,1,0:T(8,128)(2,1)S(1)} %copy-done, bf16[1,4096,128]{2,1,0:T(8,128)(2,1)S(1)} %copy-done.1, f32[512,128]{1,0:T(8,128)S(1)} %fusion.4), kind=kOutput, calls=%fused_computation.3 | convolution fusion | flops 1076232192 | bytes 10747904 | tf_op jit(solution)/shard_map/dot_general | solution.py:45
  181.8 0.1 broadcast_in_dim.109
  182.0 0.1 broadcast_in_dim.106
  182.1 80.8 %reduce-scatter.2.cloned.1.call-done = bf16[512,256]{1,0:T(8,128)(2,1)} async-done(((bf16[512,4096]{1,0:T(8,128)(2,1)}), bf16[512,256]{1,0:T(8,128)(2,1)}) %reduce-scatter.2.cloned.1.call-update) | async-done | bytes 262160 | tf_op jit(solution)/shard_map/reduce_scatter | solution.py:57
  262.9 1.5 gather_fusion.1
  264.4 1.0 select_convert_fusion
  265.5 21.9 %all-to-all-start = ((bf16[32,32,256]{2,1,0:T(8,128)(2,1)}), bf16[32,32,256]{2,1,0:T(8,128)(2,1)S(1)}, u32[]{:S(2)}, u32[]{:S(2)}) async-start(bf16[32,32,256]{2,1,0:T(8,128)(2,1)} %select_convert_fusion), calls=%async_computation.1 | async-start | bytes 1048576 | tf_op jit(solution)/shard_map/all_to_all | solution.py:66
  287.4 0.1 copy.12
  287.5 0.6 gather_fusion.2
  288.3 17.3 %all-to-all-done = bf16[32,32,256]{2,1,0:T(8,128)(2,1)S(1)} async-done(((bf16[32,32,256]{2,1,0:T(8,128)(2,1)}), bf16[32,32,256]{2,1,0:T(8,128)(2,1)S(1)}, u32[]{:S(2)}, u32[]{:S(2)}) %all-to-all-start) | async-done | bytes 524320 | tf_op jit(solution)/shard_map/all_to_all | solution.py:66
  305.6 0.8 multiply_reduce_fusion
  (30 shorter events, 0.6 us)
Async XLA Ops:
  6.5 166.5 %copy-start = (bf16[1,128,4096]{2,1,0:T(8,128)(2,1)S(1)}, bf16[1,128,4096]{2,1,0:T(8,128)(2,1)}, u32[]{:S(2)}) copy-start(bf16[1,128,4096]{2,1,0:T(8,128)(2,1)} %param.13) | copy-start | bytes 3145732
  6.5 166.5 %copy-start.1 = (bf16[1,4096,128]{2,1,0:T(8,128)(2,1)S(1)}, bf16[1,4096,128]{2,1,0:T(8,128)(2,1)}, u32[]{:S(2)}) copy-start(bf16[1,4096,128]{2,1,0:T(8,128)(2,1)} %param.12) | copy-start | bytes 3145732
  6.5 162.8 %all-gather.2.cloned.1.call-start = ((), (), s32[]{:S(2)}) async-start(), calls=%async_computation.2 | async-start | bytes 4456448 | tf_op jit(solution)/shard_map/all_gather | solution.py:41
  99.0 163.9 %reduce-scatter.2.cloned.1.call-start = ((), (), s32[]{:S(2)}) async-start(), calls=%async_computation.3 | async-start | bytes 4456448 | tf_op jit(solution)/shard_map/reduce_scatter | solution.py:57
  181.7 105.7 %copy-start.2 = (s32[8,2]{0,1:T(2,128)S(1)}, s32[8,2]{0,1:T(2,128)}, u32[]{:S(2)}) copy-start(s32[8,2]{0,1:T(2,128)} %param.10) | copy-start | bytes 196
  181.7 106.6 %copy-start.3 = (f32[32,2]{0,1:T(2,128)S(1)}, f32[32,2]{0,1:T(2,128)}, u32[]{:S(2)}) copy-start(f32[32,2]{0,1:T(2,128)} %param.9) | copy-start | bytes 772
  265.5 40.2 %all-to-all-start = ((bf16[32,32,256]{2,1,0:T(8,128)(2,1)}), bf16[32,32,256]{2,1,0:T(8,128)(2,1)S(1)}, u32[]{:S(2)}, u32[]{:S(2)}) async-start(bf16[32,32,256]{2,1,0:T(8,128)(2,1)} %select_convert_fusion), calls=%async_computation.1 | async-start | bytes 1048576 | tf_op jit(solution)/shard_map/all_to_all | solution.py:66
Sparse Core Ops, SparseCore 0:
  99.1 70.1 all-gather.1
  181.8 81.0 reduce-scatter.1
where the time goes:
time: 314 us; the launch traced here: 313 us
  waiting for transfers between devices  168 us (54%)
  blocking collectives  87.3 us (28%)
  starting transfers between devices  22 us (7%)
  between operations  13.5 us (4%)
  matrix products  12.4 us (4%)
  other arithmetic  6.52 us (2%)
  local copies, waits for them, and re-layouts  3.24 us (1%)
    reduce_scatter x1, waiting for transfers between devices, per_device(): lax.psum_scatter(term_vals, ('sec', 'hid'), scatter_dimension=1, tiled=True)  80.8 us
    all_gather x1, waiting for transfers between devices, per_device(): lax.all_gather(picked_rows, ('sec', 'hid'), axis=1, tiled=True)  70.2 us
    all_gather x1, blocking collectives, per_device(): gathered = lax.all_gather(normed, 'exp', axis=0, tiled=True)  54.8 us
    psum x1, blocking collectives, per_device(): square_total = lax.psum(square_part, ('sec', 'hid'))  32.5 us
    all_to_all x1, starting transfers between devices, per_device(): lax.all_to_all(outgoing.astype(jnp.bfloat16), 'exp', split_axis=0, concat...  21.9 us
    all_to_all x1, waiting for transfers between devices, per_device(): lax.all_to_all(outgoing.astype(jnp.bfloat16), 'exp', split_axis=0, concat...  17.3 us
    dot_general x1, matrix products, per_device(): jnp.dot(activated, down_local, preferred_element_type=jnp.float32)  8.64 us
  transfers between devices with their start and end apart: 3, of which 3 were waited for; matrix products, arithmetic and copies ran while one was open for 0% of the time, Pallas kernels for 0%

commit v1 on v0

--- a/solution.py
+++ b/solution.py
@@ -30,7 +30,7 @@
     slot_valid = jnp.any(slot_match, axis=1)
     values = tokens.astype(jnp.float32)
     square_part = jnp.sum(values * values, axis=1)
-    square_total = lax.psum(square_part, ("sec", "hid"))
+    square_total = lax.psum(lax.psum(square_part, "sec"), "hid")
     rms_value = jnp.sqrt(square_total / D + 1e-05)
     normed = (values * norm_gain.astype(jnp.float32) / rms_value[:, None]).astype(jnp.bfloat16)
     gathered = lax.all_gather(normed, "exp", axis=0, tiled=True)

time: 314 us -> 302 us (0.962)
  blocking collectives: 87.3 us -> 74.5 us
    psum x1 -> x2, blocking collectives: 32.5 us -> 23.3 us  [per_device(): square_total = lax.psum(lax.psum(square_part, 'sec'), 'hid')]
    all_gather x1, blocking collectives: 54.8 us -> 51.2 us  [per_device(): gathered = lax.all_gather(normed, 'exp', axis=0, tiled=True)]
where the time goes in v1:
time: 302 us; the launch traced here: 301 us
  waiting for transfers between devices  170 us (56%)
  blocking collectives  74.5 us (25%)
  starting transfers between devices  21 us (7%)
  between operations  13.5 us (4%)
  matrix products  12.4 us (4%)
  other arithmetic  6.52 us (2%)
  local copies, waits for them, and re-layouts  3.24 us (1%)
    reduce_scatter x1, waiting for transfers between devices, per_device(): lax.psum_scatter(term_vals, ('sec', 'hid'), scatter_dimension=1, tiled=True)  81.7 us
    all_gather x1, waiting for transfers between devices, per_device(): lax.all_gather(picked_rows, ('sec', 'hid'), axis=1, tiled=True)  71.4 us
    all_gather x1, blocking collectives, per_device(): gathered = lax.all_gather(normed, 'exp', axis=0, tiled=True)  51.2 us
    psum x2, blocking collectives, per_device(): square_total = lax.psum(lax.psum(square_part, 'sec'), 'hid')  23.3 us
    all_to_all x1, starting transfers between devices, per_device(): lax.all_to_all(outgoing.astype(jnp.bfloat16), 'exp', split_axis=0, concat...  21 us
    all_to_all x1, waiting for transfers between devices, per_device(): lax.all_to_all(outgoing.astype(jnp.bfloat16), 'exp', split_axis=0, concat...  17.2 us
    dot_general x1, matrix products, per_device(): jnp.dot(activated, down_local, preferred_element_type=jnp.float32)  8.64 us
  transfers between devices with their start and end apart: 3, of which 3 were waited for; matrix products, arithmetic and copies ran while one was open for 0% of the time, Pallas kernels for 0%

profile of v1, /device:TPU:9, one launch (start us, length us, event | category | flops | bytes accessed | tf_op | source)
XLA Modules:
  0.0 301.4 jit_solution(3514616078091753310)
XLA Ops:
  6.5 0.8 compare_reduce_fusion
  7.4 0.2 reduce-window.4
  7.6 0.1 select_reduce_fusion.1
  7.7 0.1 fusion.16
  7.9 0.8 fusion.15
  8.7 3.8 %psum.14 = f32[32]{0:T(128)S(1)} all-reduce(f32[32]{0:T(128)S(1)} %fusion.15), channel_id=1, replica_groups=mesh['sec'=2,'exp'=32,'hid'=8] {'sec'}, use_global_device_ids=true, to_apply=%region_5.6 | all-reduce | flops 32 | bytes 256 | tf_op jit(solution)/shard_map/psum | solution.py:33
  12.5 19.5 %psum.15 = f32[32]{0:T(128)S(1)} all-reduce(f32[32]{0:T(128)S(1)} %psum.14), channel_id=1, replica_groups=mesh['sec'=2,'exp'=32,'hid'=8] {'hid'}, use_global_device_ids=true, to_apply=%region_6.7 | all-reduce | flops 32 | bytes 256 | tf_op jit(solution)/shard_map/psum | solution.py:33
  31.9 0.7 convert_element_type.37
  32.6 0.8 fusion.14
  33.4 51.2 %all_gather.6 = bf16[1024,256]{1,0:T(8,128)(2,1)S(1)} all-gather(bf16[32,256]{1,0:T(8,128)(2,1)S(1)} %fusion.14), channel_id=1, replica_groups=mesh['sec'=2,'exp'=32,'hid'=8] {'exp'}, dimensions={0}, use_global_device_ids=true | all-gather | bytes 540672 | tf_op jit(solution)/shard_map/all_gather | solution.py:36
  84.6 0.6 gather_fusion
  85.3 0.9 fusion.6
  86.3 71.4 %all-gather.2.cloned.1.call-done = bf16[512,4096]{1,0:T(8,128)(2,1)} async-done(((bf16[512,256]{1,0:T(8,128)(2,1)}), bf16[512,4096]{1,0:T(8,128)(2,1)}) %all-gather.2.cloned.1.call-update) | async-done | bytes 4194320 | tf_op jit(solution)/shard_map/all_gather | solution.py:41
  157.6 3.7 %fusion.4 = f32[512,128]{1,0:T(8,128)S(1)} fusion(bf16[512,4096]{1,0:T(8,128)(2,1)} %all-gather.2.cloned.1.call-done, bf16[1,4096,128]{2,1,0:T(8,128)(2,1)} %param.11), kind=kOutput, calls=%fused_computation.8 | convolution fusion | flops 536870912 | bytes 5505024 | tf_op jit(solution)/shard_map/dot_general | solution.py:42
  161.4 8.6 %convolution_convert_fusion = bf16[512,4096]{1,0:T(8,128)(2,1)} fusion(bf16[512,4096]{1,0:T(8,128)(2,1)} %all-gather.2.cloned.1.call-done, bf16[1,128,4096]{2,1,0:T(8,128)(2,1)S(1)} %copy-done, bf16[1,4096,128]{2,1,0:T(8,128)(2,1)S(1)} %copy-done.1, f32[512,128]{1,0:T(8,128)S(1)} %fusion.4), kind=kOutput, calls=%fused_computation.3 | convolution fusion | flops 1076232192 | bytes 10747904 | tf_op jit(solution)/shard_map/dot_general | solution.py:45
  170.1 0.1 broadcast_in_dim.109
  170.3 0.1 broadcast_in_dim.106
  170.4 81.7 %reduce-scatter.2.cloned.1.call-done = bf16[512,256]{1,0:T(8,128)(2,1)} async-done(((bf16[512,4096]{1,0:T(8,128)(2,1)}), bf16[512,256]{1,0:T(8,128)(2,1)}) %reduce-scatter.2.cloned.1.call-update) | async-done | bytes 262160 | tf_op jit(solution)/shard_map/reduce_scatter | solution.py:57
  252.1 1.5 gather_fusion.1
  253.6 1.0 select_convert_fusion
  254.6 21.0 %all-to-all-start = ((bf16[32,32,256]{2,1,0:T(8,128)(2,1)}), bf16[32,32,256]{2,1,0:T(8,128)(2,1)S(1)}, u32[]{:S(2)}, u32[]{:S(2)}) async-start(bf16[32,32,256]{2,1,0:T(8,128)(2,1)} %select_convert_fusion), calls=%async_computation.1 | async-start | bytes 1048576 | tf_op jit(solution)/shard_map/all_to_all | solution.py:66
  275.7 0.6 gather_fusion.2
  276.6 17.2 %all-to-all-done = bf16[32,32,256]{2,1,0:T(8,128)(2,1)S(1)} async-done(((bf16[32,32,256]{2,1,0:T(8,128)(2,1)}), bf16[32,32,256]{2,1,0:T(8,128)(2,1)S(1)}, u32[]{:S(2)}, u32[]{:S(2)}) %all-to-all-start) | async-done | bytes 524320 | tf_op jit(solution)/shard_map/all_to_all | solution.py:66
  293.8 0.8 multiply_reduce_fusion
  (31 shorter events, 0.7 us)
Async XLA Ops:
  6.5 154.8 %copy-start = (bf16[1,128,4096]{2,1,0:T(8,128)(2,1)S(1)}, bf16[1,128,4096]{2,1,0:T(8,128)(2,1)}, u32[]{:S(2)}) copy-start(bf16[1,128,4096]{2,1,0:T(8,128)(2,1)} %param.13) | copy-start | bytes 3145732
  6.5 154.8 %copy-start.1 = (bf16[1,4096,128]{2,1,0:T(8,128)(2,1)S(1)}, bf16[1,4096,128]{2,1,0:T(8,128)(2,1)}, u32[]{:S(2)}) copy-start(bf16[1,4096,128]{2,1,0:T(8,128)(2,1)} %param.12) | copy-start | bytes 3145732
  6.5 151.1 %all-gather.2.cloned.1.call-start = ((), (), s32[]{:S(2)}) async-start(), calls=%async_computation.2 | async-start | bytes 4456448 | tf_op jit(solution)/shard_map/all_gather | solution.py:41
  86.2 165.9 %reduce-scatter.2.cloned.1.call-start = ((), (), s32[]{:S(2)}) async-start(), calls=%async_computation.3 | async-start | bytes 4456448 | tf_op jit(solution)/shard_map/reduce_scatter | solution.py:57
  170.0 105.6 %copy-start.2 = (s32[8,2]{0,1:T(2,128)S(1)}, s32[8,2]{0,1:T(2,128)}, u32[]{:S(2)}) copy-start(s32[8,2]{0,1:T(2,128)} %param.10) | copy-start | bytes 196
  170.0 106.5 %copy-start.3 = (f32[32,2]{0,1:T(2,128)S(1)}, f32[32,2]{0,1:T(2,128)}, u32[]{:S(2)}) copy-start(f32[32,2]{0,1:T(2,128)} %param.9) | copy-start | bytes 772
  254.6 39.2 %all-to-all-start = ((bf16[32,32,256]{2,1,0:T(8,128)(2,1)}), bf16[32,32,256]{2,1,0:T(8,128)(2,1)S(1)}, u32[]{:S(2)}, u32[]{:S(2)}) async-start(bf16[32,32,256]{2,1,0:T(8,128)(2,1)} %select_convert_fusion), calls=%async_computation.1 | async-start | bytes 1048576 | tf_op jit(solution)/shard_map/all_to_all | solution.py:66
Sparse Core Ops, SparseCore 0:
  86.3 71.2 all-gather.1
  170.2 81.8 reduce-scatter.1
